TPU v7x, 32 devices: a whole 2x2x4 slice. The times are simulated.
32 devices in a mesh: layer: 8 (over y, x, core), lat: 4 (over z).
Axes of the slice: x: 2, y: 2, z: 4, core: 2. Of those that a mesh axis runs over, the one named last changes fastest.
Arguments:
- activations: bfloat16 [1536, 4096], P('layer', 'lat'), may hold values from -6 to 6
- w_enc: bfloat16 [1536, 8192], P('layer', 'lat'), may hold values from -0.15625 to 0.15625
- w_dec: bfloat16 [1536, 8192], P('layer', 'lat'), may hold values from -0.25 to 0.25
- b_enc: bfloat16 [8192], P('lat'), may hold values from -3 to 3
- b_dec: float32 [1536], P('layer'), may hold values from -3 to 3
- tile_ids: int32 [4, 4], replicated, may hold values from -1 to 63, as said below
Outputs:
- d_w_enc: bfloat16 [1536, 8192], P('layer', 'lat')
- d_w_dec: bfloat16 [1536, 8192], P('layer', 'lat')
- d_b_enc: float32 [8192], P('lat')
Inputs may be any that keep to these rules, and one draw needn't show every extreme that they name: `tile_ids`: row b lists the tiles of block b: live ids first, then -1. Live ids of a row are distinct, and no two of them share an owner id // 16. Each row has at least half of 4 (rounded up) live slots; some row has 4. One owner is named in every row.
All inputs are finite; a program needn't handle non-finite values.
Results may differ from a plain program's by a relative error of at most 0.02.
The roundings to bfloat16 on the way count: a program that leaves them out, or rounds other values in their place, can miss the bound.
Values may be sent and summed in bfloat16 or wider, within the bound.
No kernel may reach another device: no remote copies, remote signals or barrier semaphores. Data moves between devices by JAX's collectives and lax.ppermute only.
A program may use at most 64 MiB of HBM per device.

v0:
```python
import math
import jax
import jax.numpy as jnp
from jax import lax
from jax.sharding import PartitionSpec as P

TILE = 128


def rounded(value):
    return lax.optimization_barrier(value.astype(jnp.bfloat16)).astype(jnp.float32)


def local(activations, w_enc, w_dec, b_enc, b_dec, tile_ids):
    feature_count, row_count = activations.shape
    latent_count = w_enc.shape[1]
    owner_count = lax.axis_size("lat")
    tile_count = latent_count // TILE
    position = lax.axis_index("lat")
    owner_ids = jnp.where(tile_ids >= 0, tile_ids // tile_count, -1)
    matched = owner_ids == position
    local_tile = jnp.sum(jnp.where(matched, tile_ids % tile_count, 0), axis=1)
    wanted = jnp.any(matched, axis=1)
    chosen = (local_tile[:, None] == jnp.arange(tile_count)[None, :]) & wanted[:, None]
    chosen_half = chosen.astype(jnp.bfloat16)
    enc_table = w_enc.reshape(feature_count, tile_count, TILE)
    dec_table = w_dec.reshape(feature_count, tile_count, TILE)
    bias_table = b_enc.reshape(tile_count, TILE)
    enc_send = jnp.einsum(
        "rt,ftc->rfc", chosen_half, enc_table, preferred_element_type=jnp.float32
    ).astype(jnp.bfloat16)
    dec_send = jnp.einsum(
        "rt,ftc->rfc", chosen_half, dec_table, preferred_element_type=jnp.float32
    ).astype(jnp.bfloat16)
    bias_send = jnp.dot(chosen_half, bias_table, preferred_element_type=jnp.float32).astype(
        jnp.bfloat16
    )
    enc_recv, dec_recv, bias_recv = (
        lax.all_to_all(enc_send, "lat", split_axis=0, concat_axis=0, tiled=True),
        lax.all_to_all(dec_send, "lat", split_axis=0, concat_axis=0, tiled=True),
        lax.all_to_all(bias_send, "lat", split_axis=0, concat_axis=0, tiled=True),
    )
    my_list = lax.dynamic_index_in_dim(tile_ids, position, 0, keepdims=False)
    live_slot = my_list >= 0
    source = jnp.where(live_slot, my_list // tile_count, 0)
    live_half = live_slot.astype(jnp.bfloat16)
    live_float = live_slot.astype(jnp.float32)
    enc_cols = jnp.take(enc_recv, source, axis=0) * live_half[:, None, None]
    bias_cols = jnp.take(bias_recv, source, axis=0).astype(jnp.float32)
    partial_value = rounded(
        jnp.einsum("fr,kfc->rkc", activations, enc_cols, preferred_element_type=jnp.float32)
    )
    preact = lax.psum(partial_value, "layer") + bias_cols[None]
    latent_codes = (jax.nn.relu(preact) * live_float[None, :, None]).astype(jnp.bfloat16)
    dec_cols = jnp.take(dec_recv, source, axis=0) * live_half[:, None, None]
    rebuilt = (
        jnp.einsum("rkc,kfc->fr", latent_codes, dec_cols, preferred_element_type=jnp.float32)
        + b_dec[:, None]
    )
    residual = rebuilt - activations.astype(jnp.float32)
    grad_err = (residual / math.sqrt(row_count)).astype(jnp.bfloat16)
    dec_grad = jnp.einsum(
        "fr,rkc->kfc", grad_err, latent_codes, preferred_element_type=jnp.float32
    ).astype(jnp.bfloat16)
    back_part = rounded(
        jnp.einsum("fr,kfc->rkc", grad_err, dec_cols, preferred_element_type=jnp.float32)
    )
    grad_total = lax.psum(back_part, "layer")
    code_grad = (grad_total * (latent_codes > 0)).astype(jnp.bfloat16)
    enc_grad = jnp.einsum(
        "fr,rkc->kfc", activations, code_grad, preferred_element_type=jnp.float32
    ).astype(jnp.bfloat16)
    bias_grad = jnp.sum(code_grad, axis=0, dtype=jnp.float32).astype(jnp.bfloat16)
    placement = ((source[:, None] == jnp.arange(owner_count)[None, :]) & live_slot[:, None]).astype(
        jnp.bfloat16
    )
    enc_return = jnp.einsum(
        "ko,kfc->ofc", placement, enc_grad, preferred_element_type=jnp.float32
    ).astype(jnp.bfloat16)
    dec_return = jnp.einsum(
        "ko,kfc->ofc", placement, dec_grad, preferred_element_type=jnp.float32
    ).astype(jnp.bfloat16)
    bias_return = jnp.einsum(
        "ko,kc->oc", placement, bias_grad, preferred_element_type=jnp.float32
    ).astype(jnp.bfloat16)
    enc_got, dec_got, bias_got = (
        lax.all_to_all(enc_return, "lat", split_axis=0, concat_axis=0, tiled=True),
        lax.all_to_all(dec_return, "lat", split_axis=0, concat_axis=0, tiled=True),
        lax.all_to_all(bias_return, "lat", split_axis=0, concat_axis=0, tiled=True),
    )
    d_w_enc = (
        jnp.einsum("rt,rfc->ftc", chosen_half, enc_got, preferred_element_type=jnp.float32)
        .reshape(feature_count, latent_count)
        .astype(jnp.bfloat16)
    )
    d_w_dec = (
        jnp.einsum("rt,rfc->ftc", chosen_half, dec_got, preferred_element_type=jnp.float32)
        .reshape(feature_count, latent_count)
        .astype(jnp.bfloat16)
    )
    d_b_enc = jnp.einsum(
        "rt,rc->tc", chosen_half, bias_got, preferred_element_type=jnp.float32
    ).reshape(latent_count)
    return (d_w_enc, d_w_dec, d_b_enc)


def solution(mesh):
    return jax.shard_map(
        local,
        mesh=mesh,
        in_specs=(
            P("layer", "lat"),
            P("layer", "lat"),
            P("layer", "lat"),
            P("lat"),
            P("layer"),
            P(),
        ),
        out_specs=(P("layer", "lat"), P("layer", "lat"), P("lat")),
        check_vma=False,
    )
```

profile of v0, /device:TPU:0, one launch (start us, length us, event | category | flops | bytes accessed | tf_op | source)
XLA Modules:
  0.0 188.2 jit_solution(17841347270297134224)
XLA Ops:
  7.2 0.9 fusion.44
  8.1 0.8 fusion.23
  9.7 6.3 %all-to-all-start.1 = ((bf16[4,1,128]{2,1,0:T(2,128)(2,1)}), bf16[4,1,128]{2,1,0:T(2,128)(2,1)S(1)}, u32[]{:S(2)}, u32[]{:S(2)}) async-start(bf16[4,1,128]{2,1,0:T(2,128)(2,1)} %copy.46), calls=%async_computation.1 | async-start | bytes 4096 | tf_op jit(solution)/shard_map/all_to_all | solution.py:41
  16.7 0.7 compare_and_fusion
  17.5 1.3 copy.65
  21.6 5.1 %all-to-all-start = ((bf16[4,192,128]{2,1,0:T(8,128)(2,1)}), bf16[4,192,128]{2,1,0:T(8,128)(2,1)S(1)}, u32[]{:S(2)}, u32[]{:S(2)}) async-start(bf16[4,192,128]{2,1,0:T(8,128)(2,1)} %copy.45), calls=%async_computation | async-start | bytes 393216 | tf_op jit(solution)/shard_map/all_to_all | solution.py:39
  27.3 6.6 %all-to-all-done = bf16[4,192,128]{2,1,0:T(8,128)(2,1)S(1)} async-done(((bf16[4,192,128]{2,1,0:T(8,128)(2,1)}), bf16[4,192,128]{2,1,0:T(8,128)(2,1)S(1)}, u32[]{:S(2)}, u32[]{:S(2)}) %all-to-all-start) | async-done | bytes 196640 | tf_op jit(solution)/shard_map/all_to_all | solution.py:39
  34.0 3.4 %all-to-all-start.2 = ((bf16[4,192,128]{2,1,0:T(8,128)(2,1)}), bf16[4,192,128]{2,1,0:T(8,128)(2,1)S(1)}, u32[]{:S(2)}, u32[]{:S(2)}) async-start(bf16[4,192,128]{2,1,0:T(8,128)(2,1)} %copy.47), calls=%async_computation.2 | async-start | bytes 393216 | tf_op jit(solution)/shard_map/all_to_all | solution.py:40
  38.6 56.5 %all-reduce.4 = f32[1024,4,128]{0,2,1:T(8,128)S(1)} all-reduce(bf16[1024,4,128]{0,2,1:T(8,128)(2,1)S(1)} %fusion), channel_id=1, replica_groups=mesh['layer'=8,'lat'=4] {'layer'}, use_global_device_ids=true, to_apply=%region_2.4 | all-reduce | flops 524288 | bytes 3145728 | tf_op jit(solution)/shard_map/psum | solution.py:53
  95.4 1.2 gather_fusion.2
  96.7 1.6 fusion.5
  98.3 1.6 convolution_convert_fusion
  100.4 1.0 convolution_convert_fusion.8
  101.4 0.7 copy.56
  102.1 5.0 %all-to-all-start.4 = ((bf16[4,192,128]{2,1,0:T(8,128)(2,1)}), bf16[4,192,128]{2,1,0:T(8,128)(2,1)S(1)}, u32[]{:S(2)}, u32[]{:S(2)}) async-start(bf16[4,192,128]{2,1,0:T(8,128)(2,1)} %copy.56), calls=%async_computation.4 | async-start | bytes 393216 | tf_op jit(solution)/shard_map/all_to_all | solution.py:88
  107.1 49.9 %all-reduce.3.cloned.1.call-done = bf16[1024,4,128]{0,2,1:T(8,128)(2,1)} async-done(((bf16[1024,4,128]{0,2,1:T(8,128)(2,1)}), bf16[1024,4,128]{0,2,1:T(8,128)(2,1)}) %all-reduce.3.cloned.1.call-update) | async-done | bytes 1048592 | tf_op jit(solution)/shard_map/psum | solution.py:68
  157.0 2.0 %fusion.41 = bf16[4,128]{1,0:T(4,128)(2,1)S(1)} fusion(bf16[1024,4,128]{0,2,1:T(8,128)(2,1)} %all-reduce.3.cloned.1.call-done, f32[4]{0:T(128)S(1)} %copy-done.9, f32[1024,4,128]{0,2,1:T(8,128)S(1)} %all-reduce.4, f32[4,128]{1,0:T(4,128)S(1)} %select_convert_fusion.1), kind=kLoop, calls=%fused_computation.90 | loop fusion | flops 4718080 | bytes 3148816 | tf_op jit(solution)/shard_map/reduce_sum | solution.py:73
  160.2 4.5 %all-to-all-start.5 = ((bf16[4,1,128]{2,1,0:T(2,128)(2,1)}), bf16[4,1,128]{2,1,0:T(2,128)(2,1)S(1)}, u32[]{:S(2)}, u32[]{:S(2)}) async-start(bf16[4,1,128]{2,1,0:T(2,128)(2,1)} %copy.58), calls=%async_computation.5 | async-start | bytes 4096 | tf_op jit(solution)/shard_map/all_to_all | solution.py:89
  165.7 4.5 %all-to-all-done.5 = bf16[4,1,128]{2,1,0:T(2,128)(2,1)S(1)} async-done(((bf16[4,1,128]{2,1,0:T(2,128)(2,1)}), bf16[4,1,128]{2,1,0:T(2,128)(2,1)S(1)}, u32[]{:S(2)}, u32[]{:S(2)}) %all-to-all-start.5) | async-done | bytes 1056 | tf_op jit(solution)/shard_map/all_to_all | solution.py:89
  170.2 3.4 %all-to-all-start.3 = ((bf16[4,192,128]{2,1,0:T(8,128)(2,1)}), bf16[4,192,128]{2,1,0:T(8,128)(2,1)S(1)}, u32[]{:S(2)}, u32[]{:S(2)}) async-start(bf16[4,192,128]{2,1,0:T(8,128)(2,1)} %copy.52), calls=%async_computation.3 | async-start | bytes 393216 | tf_op jit(solution)/shard_map/all_to_all | solution.py:87
  174.0 1.1 copy.84
  175.1 0.8 convolution_bitcast_fusion.1
  175.9 3.9 %all-to-all-done.3 = bf16[4,192,128]{2,1,0:T(8,128)(2,1)S(1)} async-done(((bf16[4,192,128]{2,1,0:T(8,128)(2,1)}), bf16[4,192,128]{2,1,0:T(8,128)(2,1)S(1)}, u32[]{:S(2)}, u32[]{:S(2)}) %all-to-all-start.3) | async-done | bytes 196640 | tf_op jit(solution)/shard_map/all_to_all | solution.py:87
  180.2 1.1 copy.85
  (60 shorter events, 10.0 us)
Async XLA Ops:
  7.2 1.8 copy-start
  7.2 11.8 %copy-start.2 = (bf16[192,2048]{1,0:T(8,128)(2,1)S(1)}, bf16[192,2048]{1,0:T(8,128)(2,1)}, u32[]{:S(2)}) copy-start(bf16[192,2048]{1,0:T(8,128)(2,1)} %param.10) | copy-start | bytes 2359300
  9.7 11.9 %all-to-all-start.1 = ((bf16[4,1,128]{2,1,0:T(2,128)(2,1)}), bf16[4,1,128]{2,1,0:T(2,128)(2,1)S(1)}, u32[]{:S(2)}, u32[]{:S(2)}) async-start(bf16[4,1,128]{2,1,0:T(2,128)(2,1)} %copy.46), calls=%async_computation.1 | async-start | bytes 4096 | tf_op jit(solution)/shard_map/all_to_all | solution.py:41
  16.7 2.8 %copy-start.10 = (pred[4]{0:T(512)(128)(4,1)}, pred[4]{0:T(512)(128)(4,1)S(1)}, u32[]{:S(2)}) copy-start(pred[4]{0:T(512)(128)(4,1)S(1)} %get-tuple-element.5) | copy-start | bytes 16
  16.7 78.4 %copy-start.8 = (f32[4]{0:T(128)}, f32[4]{0:T(128)S(1)}, u32[]{:S(2)}) copy-start(f32[4]{0:T(128)S(1)} %get-tuple-element.4) | copy-start | bytes 52
  17.4 1.8 copy-start.12
  17.4 78.0 %copy-start.6 = (bf16[4]{0:T(256)(128)(2,1)}, bf16[4]{0:T(256)(128)(2,1)S(1)}, u32[]{:S(2)}) copy-start(bf16[4]{0:T(256)(128)(2,1)S(1)} %get-tuple-element.10) | copy-start | bytes 28
  19.0 19.0 %copy-start.4 = (bf16[192,1024]{1,0:T(8,128)(2,1)S(1)}, bf16[192,1024]{1,0:T(8,128)(2,1)}, u32[]{:S(2)}) copy-start(bf16[192,1024]{1,0:T(8,128)(2,1)} %param.8) | copy-start | bytes 1179652
  21.6 12.4 %all-to-all-start = ((bf16[4,192,128]{2,1,0:T(8,128)(2,1)}), bf16[4,192,128]{2,1,0:T(8,128)(2,1)S(1)}, u32[]{:S(2)}, u32[]{:S(2)}) async-start(bf16[4,192,128]{2,1,0:T(8,128)(2,1)} %copy.45), calls=%async_computation | async-start | bytes 393216 | tf_op jit(solution)/shard_map/all_to_all | solution.py:39
  34.0 61.4 %all-to-all-start.2 = ((bf16[4,192,128]{2,1,0:T(8,128)(2,1)}), bf16[4,192,128]{2,1,0:T(8,128)(2,1)S(1)}, u32[]{:S(2)}, u32[]{:S(2)}) async-start(bf16[4,192,128]{2,1,0:T(8,128)(2,1)} %copy.47), calls=%async_computation.2 | async-start | bytes 393216 | tf_op jit(solution)/shard_map/all_to_all | solution.py:40
  37.3 119.6 %all-reduce.3.cloned.1.call-start = ((), (), s32[]{:S(2)}) async-start(), calls=%async_computation.6 | async-start | bytes 2097152 | tf_op jit(solution)/shard_map/psum | solution.py:68
  96.7 1.6 copy-start.3
  96.7 1.6 copy-start.7
  99.9 57.1 %copy-start.9 = (f32[4]{0:T(128)S(1)}, f32[4]{0:T(128)}, u32[]{:S(2)}) copy-start(f32[4]{0:T(128)} %copy-done.8) | copy-start | bytes 52
  100.4 58.5 %copy-start.11 = (pred[4]{0:T(512)(128)(4,1)S(1)}, pred[4]{0:T(512)(128)(4,1)}, u32[]{:S(2)}) copy-start(pred[4]{0:T(512)(128)(4,1)} %copy-done.10) | copy-start | bytes 16
  100.4 58.5 %copy-start.13 = (s32[4]{0:T(128)S(1)}, s32[4]{0:T(128)}, u32[]{:S(2)}) copy-start(s32[4]{0:T(128)} %copy-done.12) | copy-start | bytes 52
  102.1 58.1 %all-to-all-start.4 = ((bf16[4,192,128]{2,1,0:T(8,128)(2,1)}), bf16[4,192,128]{2,1,0:T(8,128)(2,1)S(1)}, u32[]{:S(2)}, u32[]{:S(2)}) async-start(bf16[4,192,128]{2,1,0:T(8,128)(2,1)} %copy.56), calls=%async_computation.4 | async-start | bytes 393216 | tf_op jit(solution)/shard_map/all_to_all | solution.py:88
  156.9 2.7 %copy-start.1 = (bf16[1024,4,128]{0,2,1:T(8,128)(2,1)S(1)}, bf16[1024,4,128]{0,2,1:T(8,128)(2,1)}, u32[]{:S(2)}) copy-start(bf16[1024,4,128]{0,2,1:T(8,128)(2,1)} %all-reduce.3.cloned.1.call-done) | copy-start | bytes 3145732
  156.9 2.7 %copy-start.5 = (bf16[192,1024]{1,0:T(8,128)(2,1)S(1)}, bf16[192,1024]{1,0:T(8,128)(2,1)}, u32[]{:S(2)}) copy-start(bf16[192,1024]{1,0:T(8,128)(2,1)} %param.8) | copy-start | bytes 1179652
  160.2 10.0 %all-to-all-start.5 = ((bf16[4,1,128]{2,1,0:T(2,128)(2,1)}), bf16[4,1,128]{2,1,0:T(2,128)(2,1)S(1)}, u32[]{:S(2)}, u32[]{:S(2)}) async-start(bf16[4,1,128]{2,1,0:T(2,128)(2,1)} %copy.58), calls=%async_computation.5 | async-start | bytes 4096 | tf_op jit(solution)/shard_map/all_to_all | solution.py:89
  170.2 9.6 %all-to-all-start.3 = ((bf16[4,192,128]{2,1,0:T(8,128)(2,1)}), bf16[4,192,128]{2,1,0:T(8,128)(2,1)S(1)}, u32[]{:S(2)}, u32[]{:S(2)}) async-start(bf16[4,192,128]{2,1,0:T(8,128)(2,1)} %copy.52), calls=%async_computation.3 | async-start | bytes 393216 | tf_op jit(solution)/shard_map/all_to_all | solution.py:87
Sparse Core Ops, SparseCore 0:
  100.0 56.8 all-reduce.2
where the time goes:
time: 189 us; the launch traced here: 188 us
  waiting for transfers between devices  65 us (34%)
  blocking collectives  56.5 us (30%)
  starting transfers between devices  27.7 us (15%)
  between operations  14.3 us (8%)
  local copies, waits for them, and re-layouts  10.1 us (5%)
  matrix products  8.36 us (4%)
  other arithmetic  6.22 us (3%)
    psum x1, blocking collectives, local(): preact = lax.psum(partial_value, 'layer') + bias_cols[None]  56.5 us
    psum x1, waiting for transfers between devices, local(): grad_total = lax.psum(back_part, 'layer')  49.9 us
    all_to_all x1, waiting for transfers between devices, local(): lax.all_to_all(enc_send, 'lat', split_axis=0, concat_axis=0, tiled=True)  6.63 us
    all_to_all x1, starting transfers between devices, local(): lax.all_to_all(bias_send, 'lat', split_axis=0, concat_axis=0, tiled=True)  6.35 us
    all_to_all x1, starting transfers between devices, local(): lax.all_to_all(enc_send, 'lat', split_axis=0, concat_axis=0, tiled=True)  5.09 us
    all_to_all x1, starting transfers between devices, local(): lax.all_to_all(dec_return, 'lat', split_axis=0, concat_axis=0, tiled=True)  4.97 us
    all_to_all x1, starting transfers between devices, local(): lax.all_to_all(bias_return, 'lat', split_axis=0, concat_axis=0, tiled=True)  4.55 us
    all_to_all x1, waiting for transfers between devices, local(): lax.all_to_all(bias_return, 'lat', split_axis=0, concat_axis=0, tiled=True)  4.53 us
  transfers between devices with their start and end apart: 7, of which 4 were waited for; matrix products, arithmetic and copies ran while one was open for 9% of the time, Pallas kernels for 0%

commit v1 on v0

--- a/solution.py
+++ b/solution.py
@@ -65,7 +65,11 @@
     back_part = rounded(
         jnp.einsum("fr,kfc->rkc", grad_err, dec_cols, preferred_element_type=jnp.float32)
     )
-    grad_total = lax.psum(back_part, "layer")
+    grad_total = back_part
+    for hop in (1, 2, 4):
+        grad_total = grad_total + lax.ppermute(
+            grad_total, "layer", [(dev, dev ^ hop) for dev in range(8)]
+        )
     code_grad = (grad_total * (latent_codes > 0)).astype(jnp.bfloat16)
     enc_grad = jnp.einsum(
         "fr,rkc->kfc", activations, code_grad, preferred_element_type=jnp.float32

time: 189 us -> 224 us (1.19)
  waiting for transfers between devices: 65 us -> 106 us
  between operations: 14.3 us -> 0.99 us
  other arithmetic: 6.22 us -> 10.8 us
  starting transfers between devices: 27.7 us -> 31 us
    ppermute x0 -> x3, waiting for transfers between devices: none -> 90.4 us  [local(): lax.ppermute(grad_total, 'layer', [(dev, dev ^ hop) for dev in range(8)])]
    psum x1 -> x0, waiting for transfers between devices: 49.9 us -> none  [local(): grad_total = lax.psum(back_part, 'layer')]
  transfers between devices with their start and end apart: 7 -> 9, of which waited for: 4 -> 6; matrix products, arithmetic and copies ran while one was open for 9% -> 8% of each run, Pallas kernels for 0% -> 0%
where the time goes in v1:
time: 224 us; the launch traced here: 223 us
  waiting for transfers between devices  106 us (47%)
  blocking collectives  56.5 us (25%)
  starting transfers between devices  31 us (14%)
  local copies, waits for them, and re-layouts  11.6 us (5%)
  other arithmetic  10.8 us (5%)
  matrix products  7.07 us (3%)
    ppermute x3, waiting for transfers between devices, local(): lax.ppermute(grad_total, 'layer', [(dev, dev ^ hop) for dev in range(8)])  90.4 us
    psum x1, blocking collectives, local(): preact = lax.psum(partial_value, 'layer') + bias_cols[None]  56.5 us
    all_to_all x1, waiting for transfers between devices, local(): lax.all_to_all(enc_send, 'lat', split_axis=0, concat_axis=0, tiled=True)  6.62 us
    all_to_all x1, starting transfers between devices, local(): lax.all_to_all(bias_send, 'lat', split_axis=0, concat_axis=0, tiled=True)  6.35 us
    all_to_all x1, starting transfers between devices, local(): lax.all_to_all(enc_send, 'lat', split_axis=0, concat_axis=0, tiled=True)  5.09 us
    all_to_all x1, starting transfers between devices, local(): lax.all_to_all(bias_return, 'lat', split_axis=0, concat_axis=0, tiled=True)  5.02 us
    all_to_all x1, starting transfers between devices, local(): lax.all_to_all(dec_return, 'lat', split_axis=0, concat_axis=0, tiled=True)  4.96 us
    all_to_all x1, waiting for transfers between devices, local(): lax.all_to_all(bias_return, 'lat', split_axis=0, concat_axis=0, tiled=True)  4.53 us
  transfers between devices with their start and end apart: 9, of which 6 were waited for; matrix products, arithmetic and copies ran while one was open for 8% of the time, Pallas kernels for 0%

profile of v1, /device:TPU:0, one launch (start us, length us, event | category | flops | bytes accessed | tf_op | source)
XLA Modules:
  0.0 223.5 jit_solution(18399068732275928717)
XLA Ops:
  3.1 6.3 %all-to-all-start.1 = ((bf16[4,1,128]{2,1,0:T(2,128)(2,1)}), bf16[4,1,128]{2,1,0:T(2,128)(2,1)S(1)}, u32[]{:S(2)}, u32[]{:S(2)}) async-start(bf16[4,1,128]{2,1,0:T(2,128)(2,1)} %copy.46), calls=%async_computation.1 | async-start | bytes 4096 | tf_op jit(solution)/shard_map/all_to_all | solution.py:41
  9.5 1.3 fusion.42
  12.1 1.3 copy.65
  16.2 5.1 %all-to-all-start = ((bf16[4,192,128]{2,1,0:T(8,128)(2,1)}), bf16[4,192,128]{2,1,0:T(8,128)(2,1)S(1)}, u32[]{:S(2)}, u32[]{:S(2)}) async-start(bf16[4,192,128]{2,1,0:T(8,128)(2,1)} %copy.45), calls=%async_computation | async-start | bytes 393216 | tf_op jit(solution)/shard_map/all_to_all | solution.py:39
  21.9 6.6 %all-to-all-done = bf16[4,192,128]{2,1,0:T(8,128)(2,1)S(1)} async-done(((bf16[4,192,128]{2,1,0:T(8,128)(2,1)}), bf16[4,192,128]{2,1,0:T(8,128)(2,1)S(1)}, u32[]{:S(2)}, u32[]{:S(2)}) %all-to-all-start) | async-done | bytes 196640 | tf_op jit(solution)/shard_map/all_to_all | solution.py:39
  28.5 4.0 %all-to-all-start.2 = ((bf16[4,192,128]{2,1,0:T(8,128)(2,1)}), bf16[4,192,128]{2,1,0:T(8,128)(2,1)}, u32[]{:S(2)}, u32[]{:S(2)}) async-start(bf16[4,192,128]{2,1,0:T(8,128)(2,1)} %copy.47), calls=%async_computation.2 | async-start | bytes 393216 | tf_op jit(solution)/shard_map/all_to_all | solution.py:40
  33.7 56.5 %all-reduce.1 = f32[1024,4,128]{0,2,1:T(8,128)S(1)} all-reduce(bf16[1024,4,128]{0,2,1:T(8,128)(2,1)S(1)} %fusion), channel_id=1, replica_groups=mesh['layer'=8,'lat'=4] {'layer'}, use_global_device_ids=true, to_apply=%region_2.4 | all-reduce | flops 524288 | bytes 3145728 | tf_op jit(solution)/shard_map/psum | solution.py:53
  90.3 1.0 multiply_convert_fusion
  91.3 2.3 %gather_fusion.2 = bf16[4,192,128]{2,1,0:T(8,128)(2,1)} fusion(bf16[4,192,128]{2,1,0:T(8,128)(2,1)} %all-to-all-done.2, s32[1024]{0:T(1024)} %copy-done.4), kind=kCustom, calls=%fused_computation.1.clone | custom fusion | bytes 393232 | tf_op jit(solution)/shard_map/jit(_take)/gather | solution.py:55
  93.6 1.4 fusion.5
  95.0 1.2 convolution_convert_fusion
  96.5 4.1 %collective-permute-done = f32[1024,4,128]{0,2,1:T(8,128)S(1)} collective-permute-done((f32[1024,4,128]{0,2,1:T(8,128)S(1)}, f32[1024,4,128]{0,2,1:T(8,128)S(1)}, u32[]{:S(2)}, u32[]{:S(2)}) %collective-permute-start) | collective-permute-done | bytes 2097184 | tf_op jit(solution)/shard_map/ppermute | solution.py:70
  102.0 46.8 %collective-permute-done.1 = f32[1024,4,128]{0,2,1:T(8,128)S(1)} collective-permute-done((f32[1024,4,128]{0,2,1:T(8,128)S(1)}, f32[1024,4,128]{0,2,1:T(8,128)S(1)}, u32[]{:S(2)}, u32[]{:S(2)}) %collective-permute-start.1) | collective-permute-done | bytes 2097184 | tf_op jit(solution)/shard_map/ppermute | solution.py:70
  148.9 1.7 add.78
  150.6 1.2 collective-permute-start.2
  153.3 5.0 %all-to-all-start.4 = ((bf16[4,192,128]{2,1,0:T(8,128)(2,1)}), bf16[4,192,128]{2,1,0:T(8,128)(2,1)S(1)}, u32[]{:S(2)}, u32[]{:S(2)}) async-start(bf16[4,192,128]{2,1,0:T(8,128)(2,1)} %copy.56), calls=%async_computation.4 | async-start | bytes 393216 | tf_op jit(solution)/shard_map/all_to_all | solution.py:92
  158.3 39.4 %collective-permute-done.2 = f32[1024,4,128]{0,2,1:T(8,128)} collective-permute-done((f32[1024,4,128]{0,2,1:T(8,128)}, f32[1024,4,128]{0,2,1:T(8,128)}, u32[]{:S(2)}, u32[]{:S(2)}) %collective-permute-start.2) | collective-permute-done | bytes 2097184 | tf_op jit(solution)/shard_map/ppermute | solution.py:70
  197.7 2.9 %fusion.41 = (bf16[4,128]{1,0:T(4,128)(2,1)S(1)}, bf16[1024,4,128]{0,2,1:T(8,128)(2,1)S(1)}) fusion(f32[1024,4,128]{0,2,1:T(8,128)} %add.78, f32[1024,4,128]{0,2,1:T(8,128)} %collective-permute-done.2, f32[4]{0:T(128)S(1)} %copy-done.5, f32[1024,4,128]{0,2,1:T(8,128)S(1)} %all-reduce.1, f32[4,128]{1,0:T(4,128)S(1)} %select_convert_fusion.1), kind=kLoop, calls=%fused_computation.91 | loop fusion | flops 4718080 | bytes 7343120 | tf_op jit(solution)/shard_map/reduce_sum | solution.py:77
  201.9 5.0 %all-to-all-start.5 = ((bf16[4,1,128]{2,1,0:T(2,128)(2,1)}), bf16[4,1,128]{2,1,0:T(2,128)(2,1)S(1)}, u32[]{:S(2)}, u32[]{:S(2)}) async-start(bf16[4,1,128]{2,1,0:T(2,128)(2,1)} %copy.58), calls=%async_computation.5 | async-start | bytes 4096 | tf_op jit(solution)/shard_map/all_to_all | solution.py:93
  207.8 4.5 %all-to-all-done.5 = bf16[4,1,128]{2,1,0:T(2,128)(2,1)S(1)} async-done(((bf16[4,1,128]{2,1,0:T(2,128)(2,1)}), bf16[4,1,128]{2,1,0:T(2,128)(2,1)S(1)}, u32[]{:S(2)}, u32[]{:S(2)}) %all-to-all-start.5) | async-done | bytes 1056 | tf_op jit(solution)/shard_map/all_to_all | solution.py:93
  212.4 3.4 %all-to-all-start.3 = ((bf16[4,192,128]{2,1,0:T(8,128)(2,1)}), bf16[4,192,128]{2,1,0:T(8,128)(2,1)S(1)}, u32[]{:S(2)}, u32[]{:S(2)}) async-start(bf16[4,192,128]{2,1,0:T(8,128)(2,1)} %copy.52), calls=%async_computation.3 | async-start | bytes 393216 | tf_op jit(solution)/shard_map/all_to_all | solution.py:91
  216.2 1.1 copy.84
  218.0 3.9 %all-to-all-done.3 = bf16[4,192,128]{2,1,0:T(8,128)(2,1)S(1)} async-done(((bf16[4,192,128]{2,1,0:T(8,128)(2,1)}), bf16[4,192,128]{2,1,0:T(8,128)(2,1)S(1)}, u32[]{:S(2)}, u32[]{:S(2)}) %all-to-all-start.3) | async-done | bytes 196640 | tf_op jit(solution)/shard_map/all_to_all | solution.py:91
  222.4 1.1 copy.85
  (64 shorter events, 15.2 us)
Async XLA Ops:
  0.6 1.8 copy-start
  0.6 13.0 %copy-start.2 = (bf16[192,2048]{1,0:T(8,128)(2,1)S(1)}, bf16[192,2048]{1,0:T(8,128)(2,1)}, u32[]{:S(2)}) copy-start(bf16[192,2048]{1,0:T(8,128)(2,1)} %param.10) | copy-start | bytes 2359300
  3.1 13.0 %all-to-all-start.1 = ((bf16[4,1,128]{2,1,0:T(2,128)(2,1)}), bf16[4,1,128]{2,1,0:T(2,128)(2,1)S(1)}, u32[]{:S(2)}, u32[]{:S(2)}) async-start(bf16[4,1,128]{2,1,0:T(2,128)(2,1)} %copy.46), calls=%async_computation.1 | async-start | bytes 4096 | tf_op jit(solution)/shard_map/all_to_all | solution.py:41
  10.8 0.7 copy-start.7
  11.5 0.6 copy-start.10
  11.5 21.7 %copy-start.6 = (bf16[4]{0:T(256)(128)(2,1)}, bf16[4]{0:T(256)(128)(2,1)S(1)}, u32[]{:S(2)}) copy-start(bf16[4]{0:T(256)(128)(2,1)S(1)} %get-tuple-element.12) | copy-start | bytes 28
  12.1 20.5 %copy-start.4 = (s32[1024]{0:T(1024)}, s32[1024]{0:T(1024)S(1)}, u32[]{:S(2)}) copy-start(s32[1024]{0:T(1024)S(1)} %pad_clamp_fusion.1) | copy-start | bytes 12292
  13.6 19.5 %copy-start.1 = (bf16[192,1024]{1,0:T(8,128)(2,1)S(1)}, bf16[192,1024]{1,0:T(8,128)(2,1)}, u32[]{:S(2)}) copy-start(bf16[192,1024]{1,0:T(8,128)(2,1)} %param.8) | copy-start | bytes 1179652
  16.2 12.4 %all-to-all-start = ((bf16[4,192,128]{2,1,0:T(8,128)(2,1)}), bf16[4,192,128]{2,1,0:T(8,128)(2,1)S(1)}, u32[]{:S(2)}, u32[]{:S(2)}) async-start(bf16[4,192,128]{2,1,0:T(8,128)(2,1)} %copy.45), calls=%async_computation | async-start | bytes 393216 | tf_op jit(solution)/shard_map/all_to_all | solution.py:39
  28.5 62.7 %all-to-all-start.2 = ((bf16[4,192,128]{2,1,0:T(8,128)(2,1)}), bf16[4,192,128]{2,1,0:T(8,128)(2,1)}, u32[]{:S(2)}, u32[]{:S(2)}) async-start(bf16[4,192,128]{2,1,0:T(8,128)(2,1)} %copy.47), calls=%async_computation.2 | async-start | bytes 393216 | tf_op jit(solution)/shard_map/all_to_all | solution.py:40
  93.6 1.4 copy-start.3
  96.5 4.2 %collective-permute-start = (f32[1024,4,128]{0,2,1:T(8,128)S(1)}, f32[1024,4,128]{0,2,1:T(8,128)S(1)}, u32[]{:S(2)}, u32[]{:S(2)}) collective-permute-start(f32[1024,4,128]{0,2,1:T(8,128)S(1)} %convert_element_type.114), channel_id=1, source_target_pairs={{0,4},{4,0},{8,12},{12,8},{16,20},{20,16},{24,28},{28,24},{1,5},{5... | collective-permute-start | bytes 6291464 | tf_op jit(solution)/shard_map/ppermute | solution.py:70
  101.1 51.2 %copy-start.8 = (pred[4]{0:T(512)(128)(4,1)S(1)}, pred[4]{0:T(512)(128)(4,1)}, u32[]{:S(2)}) copy-start(pred[4]{0:T(512)(128)(4,1)} %copy-done.7) | copy-start | bytes 16
  101.1 51.2 %copy-start.11 = (s32[4]{0:T(128)S(1)}, s32[4]{0:T(128)}, u32[]{:S(2)}) copy-start(s32[4]{0:T(128)} %copy-done.10) | copy-start | bytes 52
  101.1 47.7 %collective-permute-start.1 = (f32[1024,4,128]{0,2,1:T(8,128)S(1)}, f32[1024,4,128]{0,2,1:T(8,128)S(1)}, u32[]{:S(2)}, u32[]{:S(2)}) collective-permute-start(f32[1024,4,128]{0,2,1:T(8,128)S(1)} %convert_add_fusion), channel_id=1, source_target_pairs={{0,8},{4,12},{8,0},{12,4},{16,24},{20,28},{24,16},{28,20},{1,9},{5... | collective-permute-start | bytes 6291464 | tf_op jit(solution)/shard_map/ppermute | solution.py:70
  150.6 47.1 %copy-start.5 = (f32[4]{0:T(128)S(1)}, f32[4]{0:T(128)}, u32[]{:S(2)}) copy-start(f32[4]{0:T(128)} %get-tuple-element.6) | copy-start | bytes 52
  150.6 47.1 %collective-permute-start.2 = (f32[1024,4,128]{0,2,1:T(8,128)}, f32[1024,4,128]{0,2,1:T(8,128)}, u32[]{:S(2)}, u32[]{:S(2)}) collective-permute-start(f32[1024,4,128]{0,2,1:T(8,128)} %add.78), channel_id=1, source_target_pairs={{0,16},{4,20},{8,24},{12,28},{16,0},{20,4},{24,8},{28,12},{1,17},{... | collective-permute-start | bytes 6291464 | tf_op jit(solution)/shard_map/ppermute | solution.py:70
  153.3 48.5 %all-to-all-start.4 = ((bf16[4,192,128]{2,1,0:T(8,128)(2,1)}), bf16[4,192,128]{2,1,0:T(8,128)(2,1)S(1)}, u32[]{:S(2)}, u32[]{:S(2)}) async-start(bf16[4,192,128]{2,1,0:T(8,128)(2,1)} %copy.56), calls=%async_computation.4 | async-start | bytes 393216 | tf_op jit(solution)/shard_map/all_to_all | solution.py:92
  158.3 42.3 %copy-start.9 = (pred[4]{0:T(512)(128)(4,1)S(1)}, pred[4]{0:T(512)(128)(4,1)}, u32[]{:S(2)}) copy-start(pred[4]{0:T(512)(128)(4,1)} %copy-done.7) | copy-start | bytes 16
  158.3 42.3 %copy-start.12 = (s32[4]{0:T(128)S(1)}, s32[4]{0:T(128)}, u32[]{:S(2)}) copy-start(s32[4]{0:T(128)} %copy-done.10) | copy-start | bytes 52
  201.9 10.5 %all-to-all-start.5 = ((bf16[4,1,128]{2,1,0:T(2,128)(2,1)}), bf16[4,1,128]{2,1,0:T(2,128)(2,1)S(1)}, u32[]{:S(2)}, u32[]{:S(2)}) async-start(bf16[4,1,128]{2,1,0:T(2,128)(2,1)} %copy.58), calls=%async_computation.5 | async-start | bytes 4096 | tf_op jit(solution)/shard_map/all_to_all | solution.py:93
  212.4 9.6 %all-to-all-start.3 = ((bf16[4,192,128]{2,1,0:T(8,128)(2,1)}), bf16[4,192,128]{2,1,0:T(8,128)(2,1)S(1)}, u32[]{:S(2)}, u32[]{:S(2)}) async-start(bf16[4,192,128]{2,1,0:T(8,128)(2,1)} %copy.52), calls=%async_computation.3 | async-start | bytes 393216 | tf_op jit(solution)/shard_map/all_to_all | solution.py:91
